TPU v7x, 256 devices: a whole 4x4x8 slice. The times are simulated.
256 devices in a mesh: gx: 16 (over x, y), gy: 16 (over z, core).
Axes of the slice: x: 4, y: 4, z: 8, core: 2. Of those that a mesh axis runs over, the one named last changes fastest.
Arguments:
- positions: float32 [3, 524288], P(None, ('gx', 'gy')), may hold values from -6 to 6
- strengths: float32 [3, 524288], P(None, ('gx', 'gy')), may hold values from -2 to 2
- cores: float32 [524288], P(('gx', 'gy')), may hold values from 0.05 to 0.5
- cell_local: int32 [524288], P(('gx', 'gy')), may hold values from 0 to 1
- cell_centers: float32 [3, 512], P(None, ('gx', 'gy')), may hold values from -6 to 6
- send_blocks: int32 [4096, 4], P(('gx', 'gy')), may hold values from 0 to 15, as said below
- pair_src: int32 [16384, 2], P(('gx', 'gy')), may hold values from 0 to 15, as said below
- counts: int32 [4096], P(('gx', 'gy')), may hold values from 1 to 4
Outputs:
- stretch_first: float32 [3, 524288], P(None, ('gx', 'gy'))
- stretch_second: float32 [3, 524288], P(None, ('gx', 'gy'))
Inputs may be any that keep to these rules, and one draw needn't show every extreme that they name: `send_blocks`: each row names 4 different blocks of the sending device. `pair_src`: each row names 2 different blocks of the partner.
All inputs are finite; a program needn't handle non-finite values.
Results may differ from a plain program's by a relative error of at most 0.0003.
Values sent between devices are 32-bit elements; how exact they have to be, the bound alone decides.
A program may use at most 64 MiB of HBM per device.

v0:
```python
import math

import jax
import jax.numpy as jnp
from jax import lax
from jax.sharding import Mesh
from jax.sharding import PartitionSpec as P

BLOCK = 128
SLOTS = 4
PAIRS = 2
CELLS_DEV = 2
GY = ("gy_0", "gy_1")
GX_GY = ("gx_0", "gx_1", "gy_0", "gy_1")
GX = ("gx_0", "gx_1")


far_core = 1.0
step_size = 0.1
inv_four_pi = 1.0 / (4.0 * math.pi)


def from_everyone(shard, axis):
    peers = lax.axis_size(axis)
    return lax.all_to_all(
        jnp.broadcast_to(shard[None], (peers, *shard.shape)), axis, 0, 0, tiled=True
    )


def in_order(parts, dim):
    parts = jnp.moveaxis(parts, 0, dim)
    shape = parts.shape
    return parts.reshape(*shape[:dim], shape[dim] * shape[dim + 1], *shape[dim + 2 :])


def gathered_by_axis(shard, axes, dim):
    far, near = axes
    parts = from_everyone(from_everyone(shard, far), near)
    return in_order(parts.swapaxes(0, 1).reshape(-1, *shard.shape), dim)


def tile_gradient(tpos, tcore, spos, salpha, score):
    rx = tpos[0][:, None] - spos[0][None, :]
    ry = tpos[1][:, None] - spos[1][None, :]
    rz = tpos[2][:, None] - spos[2][None, :]
    s2 = (
        rx * rx
        + ry * ry
        + rz * rz
        + 0.5 * (tcore[:, None] * tcore[:, None] + score[None, :] * score[None, :])
    )
    inv = lax.rsqrt(s2)
    inv3 = inv * inv * inv
    inv5 = inv3 / s2
    ax = salpha[0][None, :]
    ay = salpha[1][None, :]
    az = salpha[2][None, :]
    w0 = jnp.sum(ax * inv3, axis=1)
    w1 = jnp.sum(ay * inv3, axis=1)
    w2 = jnp.sum(az * inv3, axis=1)
    zero = jnp.zeros_like(w0)
    eps_rows = [[zero, w2, -w1], [-w2, zero, w0], [w1, -w0, zero]]
    crosses = [ry * az - rz * ay, rz * ax - rx * az, rx * ay - ry * ax]
    dists = [rx, ry, rz]
    rows = []
    for first in range(3):
        weighted = crosses[first] * inv5
        for second in range(3):
            term = jnp.sum(weighted * dists[second], axis=1)
            rows.append((3.0 * term - eps_rows[first][second]) * inv_four_pi)
    return jnp.stack(rows, axis=0)


def block_gradient(tpos, tcore, sources):
    grads = jax.vmap(
        lambda source: tile_gradient(tpos, tcore, source[0:3], source[3:6], source[6])
    )(sources)
    return jnp.sum(grads, axis=0)


def stretch_of(alpha, grad):
    rows = []
    for first in range(3):
        rows.append(
            alpha[..., 0, :] * grad[..., 3 * first, :]
            + alpha[..., 1, :] * grad[..., 3 * first + 1, :]
            + alpha[..., 2, :] * grad[..., 3 * first + 2, :]
        )
    return jnp.stack(rows, axis=-2)


def remote_terms(tpos, tcore, rows, parts):

    def per_peer(item):
        pos_one, core_one, alpha_one, rows_one = item
        sources = parts[rows_one]
        grads = jax.vmap(block_gradient)(pos_one, core_one, sources)
        return grads

    return lax.map(per_peer, (tpos, tcore, None, rows), batch_size=4)


def send_back(partial_terms):
    return lax.all_to_all(partial_terms, GY, split_axis=0, concat_axis=0, tiled=True)


def evaluate(
    positions, alpha, cores, cell_local, cell_centers, send_blocks, pair_src, counts, kept
):
    blocks = positions.shape[1] // BLOCK
    peers = lax.axis_size(GY)
    parts = jnp.concatenate([positions, alpha, cores[None, :]], axis=0)
    parts = parts.reshape(7, blocks, BLOCK).transpose(1, 0, 2)
    pair_rows = pair_src.reshape(peers, SLOTS, PAIRS)
    saved = None
    if kept is None:
        targets = parts[send_blocks]
        payload = jnp.concatenate([targets[:, :, 0:3], targets[:, :, 6:7]], axis=2)
        remote_got = lax.all_to_all(payload, GY, split_axis=0, concat_axis=0, tiled=True)
        remote_rows = lax.all_to_all(pair_rows, GY, split_axis=0, concat_axis=0, tiled=True)
        back = send_back(
            remote_terms(remote_got[:, :, 0:3], remote_got[:, :, -1], remote_rows, parts)
        )
        result = (back, remote_got, remote_rows)
        returned, got_kept, rows_kept = result
        saved = (got_kept, rows_kept)
    else:
        got, rows = kept
        returned = send_back(remote_terms(got[:, :, 0:3], got[:, :, -1], rows, parts))
    live = (jnp.arange(SLOTS, dtype=jnp.int32)[None, :] < counts[:, None]).astype(jnp.float32)
    weight = (send_blocks[:, :, None] == jnp.arange(blocks, dtype=jnp.int32)[None, None, :]).astype(
        jnp.float32
    ) * live[:, :, None]
    near = jnp.einsum("gkt,gkcb->tcb", weight, returned, precision=lax.Precision.HIGHEST)
    cell_hot = (
        cell_local.reshape(blocks, BLOCK)[:, :, None]
        == jnp.arange(CELLS_DEV, dtype=jnp.int32)[None, None, :]
    ).astype(jnp.float32)
    gamma = jnp.einsum("tcb,tbk->ck", parts[:, 3:6, :], cell_hot, precision=lax.Precision.HIGHEST)
    all_gamma, all_centers = (
        gathered_by_axis(gamma, ("gx_0", ("gx_1", "gy_0", "gy_1")), 1),
        gathered_by_axis(cell_centers, ("gx_0", ("gx_1", "gy_0", "gy_1")), 1),
    )
    total_cells = all_gamma.shape[1]
    device_index = lax.axis_index(GX) * peers + lax.axis_index(GY)
    keep = (jnp.arange(total_cells, dtype=jnp.int32) // CELLS_DEV != device_index).astype(
        jnp.float32
    )
    far_gamma = all_gamma * keep[None, :]
    far_cores = jnp.full((total_cells,), far_core, dtype=jnp.float32)
    far = lax.map(
        lambda target: tile_gradient(target[0:3], target[6], all_centers, far_gamma, far_cores),
        parts,
        batch_size=4,
    )
    alpha_blocks = parts[:, 3:6, :]
    stretch = stretch_of(alpha_blocks, near + far)
    return (stretch.transpose(1, 0, 2).reshape(3, blocks * BLOCK), saved)


def body(positions, strengths, cores, cell_local, cell_centers, send_blocks, pair_src, counts):
    stretch_first, saved = evaluate(
        positions, strengths, cores, cell_local, cell_centers, send_blocks, pair_src, counts, None
    )
    moved = strengths + step_size * stretch_first
    stretch_second, unused_saved = evaluate(
        positions, moved, cores, cell_local, cell_centers, send_blocks, pair_src, counts, saved
    )
    return (stretch_first, stretch_second)


def solution(mesh):
    finer = Mesh(mesh.devices.reshape(4, 4, 8, 2), ("gx_0", "gx_1", "gy_0", "gy_1"))
    placed = (
        P(None, GX_GY),
        P(None, GX_GY),
        P(GX_GY),
        P(GX_GY),
        P(None, GX_GY),
        P(GX_GY, None),
        P(GX_GY, None),
        P(GX_GY),
    )
    return jax.shard_map(
        body,
        mesh=finer,
        in_specs=placed,
        out_specs=(P(None, GX_GY), P(None, GX_GY)),
        check_vma=False,
    )
```

profile of v0, /device:TPU:1, one launch (start us, length us, event | category | flops | bytes accessed | tf_op | source)
XLA Modules:
  0.0 232.5 jit_solution(15643870634721380089)
XLA Ops:
  0.7 0.8 copy_bitcast_fusion.3
  1.5 0.7 fusion.120
  2.2 0.8 convolution_bitcast_fusion.3
  3.0 0.7 broadcast_in_dim.55
  3.7 4.8 %all-to-all-start.5 = ((f32[4,3,2]{1,2,0:T(2,128)}), f32[4,3,2]{1,2,0:T(2,128)S(1)}, u32[]{:S(2)}, u32[]{:S(2)}) async-start(f32[4,3,2]{1,2,0:T(2,128)} %broadcast_in_dim.55), calls=%async_computation.5 | async-start | bytes 8192 | tf_op jit(solution)/shard_map/all_to_all | solution.py:25
  8.6 4.0 %all-to-all-done.5 = f32[4,3,2]{1,2,0:T(2,128)S(1)} async-done(((f32[4,3,2]{1,2,0:T(2,128)}), f32[4,3,2]{1,2,0:T(2,128)S(1)}, u32[]{:S(2)}, u32[]{:S(2)}) %all-to-all-start.5) | async-done | bytes 128 | tf_op jit(solution)/shard_map/all_to_all | solution.py:25
  12.7 0.6 broadcast_in_dim.53
  13.2 3.2 %all-to-all-start.3 = ((f32[4,3,2]{1,2,0:T(2,128)}), f32[4,3,2]{1,2,0:T(2,128)S(1)}, u32[]{:S(2)}, u32[]{:S(2)}) async-start(f32[4,3,2]{1,2,0:T(2,128)} %broadcast_in_dim.53), calls=%async_computation.3 | async-start | bytes 8192 | tf_op jit(solution)/shard_map/all_to_all | solution.py:25
  16.5 0.6 copy.233
  17.1 3.5 %all-to-all-done.3 = f32[4,3,2]{1,2,0:T(2,128)S(1)} async-done(((f32[4,3,2]{1,2,0:T(2,128)}), f32[4,3,2]{1,2,0:T(2,128)S(1)}, u32[]{:S(2)}, u32[]{:S(2)}) %all-to-all-start.3) | async-done | bytes 128 | tf_op jit(solution)/shard_map/all_to_all | solution.py:25
  20.6 11.7 %all-to-all-start.1 = ((s32[16,4,2]{1,2,0:T(2,128)}), s32[16,4,2]{1,2,0:T(2,128)S(1)}, u32[]{:S(2)}, u32[]{:S(2)}) async-start(s32[16,4,2]{1,2,0:T(2,128)} %copy.233), calls=%async_computation.1 | async-start | bytes 32768 | tf_op jit(solution)/shard_map/all_to_all | solution.py:120
  32.6 7.0 %all-to-all-done.1 = s32[16,4,2]{1,2,0:T(2,128)S(1)} async-done(((s32[16,4,2]{1,2,0:T(2,128)}), s32[16,4,2]{1,2,0:T(2,128)S(1)}, u32[]{:S(2)}, u32[]{:S(2)}) %all-to-all-start.1) | async-done | bytes 544 | tf_op jit(solution)/shard_map/all_to_all | solution.py:120
  39.7 0.7 broadcast_in_dim.56
  40.4 5.5 %all-to-all-start.6 = ((f32[64,4,3,2]{1,3,2,0:T(2,128)}), f32[64,4,3,2]{1,3,2,0:T(2,128)S(1)}, u32[]{:S(2)}, u32[]{:S(2)}) async-start(f32[64,4,3,2]{1,3,2,0:T(2,128)} %broadcast_in_dim.56), calls=%async_computation.6 | async-start | bytes 393216 | tf_op jit(solution)/shard_map/all_to_all | solution.py:25
  46.0 0.6 gather_fusion.2
  46.8 10.1 %all-to-all-done.6 = f32[64,4,3,2]{1,3,2,0:T(2,128)S(1)} async-done(((f32[64,4,3,2]{1,3,2,0:T(2,128)}), f32[64,4,3,2]{1,3,2,0:T(2,128)S(1)}, u32[]{:S(2)}, u32[]{:S(2)}) %all-to-all-start.6) | async-done | bytes 6176 | tf_op jit(solution)/shard_map/all_to_all | solution.py:25
  56.9 0.7 broadcast_in_dim.54
  57.6 5.7 %all-to-all-start.4 = ((f32[64,4,3,2]{1,3,2,0:T(2,128)}), f32[64,4,3,2]{1,3,2,0:T(2,128)S(1)}, u32[]{:S(2)}, u32[]{:S(2)}) async-start(f32[64,4,3,2]{1,3,2,0:T(2,128)} %broadcast_in_dim.54), calls=%async_computation.4 | async-start | bytes 393216 | tf_op jit(solution)/shard_map/all_to_all | solution.py:25
  63.3 0.7 pad_maximum_fusion
  64.0 10.2 %all-to-all-done.4 = f32[64,4,3,2]{1,3,2,0:T(2,128)S(1)} async-done(((f32[64,4,3,2]{1,3,2,0:T(2,128)}), f32[64,4,3,2]{1,3,2,0:T(2,128)S(1)}, u32[]{:S(2)}, u32[]{:S(2)}) %all-to-all-start.4) | async-done | bytes 6176 | tf_op jit(solution)/shard_map/all_to_all | solution.py:25
  74.2 4.2 %all-to-all-start = ((f32[16,4,4,128]{3,2,1,0:T(4,128)}), f32[16,4,4,128]{3,2,1,0:T(4,128)S(1)}, u32[]{:S(2)}, u32[]{:S(2)}) async-start(f32[16,4,4,128]{3,2,1,0:T(4,128)} %pad_maximum_fusion), calls=%async_computation | async-start | bytes 262144 | tf_op jit(solution)/shard_map/all_to_all | solution.py:119
  79.9 7.5 %all-to-all-done = f32[16,4,4,128]{3,2,1,0:T(4,128)S(1)} async-done(((f32[16,4,4,128]{3,2,1,0:T(4,128)}), f32[16,4,4,128]{3,2,1,0:T(4,128)S(1)}, u32[]{:S(2)}, u32[]{:S(2)}) %all-to-all-start) | async-done | bytes 131104 | tf_op jit(solution)/shard_map/all_to_all | solution.py:119
  87.5 0.7 broadcast.958.clone2
  88.2 43.6 %while.52 = (s32[]{:T(128)}, f32[4,4,4,9,128]{4,2,3,1,0:T(4,128)}, f32[4,4,4,3,128]{4,2,1,3,0:T(4,128)S(1)}, s32[4,4,4,2]{2,1,3,0:T(4,128)S(1)}, f32[16,7,128]{2...) while((s32[]{:T(128)}, f32[4,4,4,9,128]{4,2,3,1,0:T(4,128)}, ...), condition=%wide.region_14.15_spmd, body=%wide.region_0.14_spmd.sunk | while | flops 26289248 | bytes 1685093 | solution.py:100
  89.2 8.9 %fusion.142 = (f32[4,4,2,128]{3,2,1,0:T(2,128)S(1)}, f32[4,4,2,128]{3,2,1,0:T(2,128)S(1)}, f32[4,4,2,128]{3,2,1,0:T(2,128)S(1)}, f32[4,4,2,128]{3,2,1,0:T(2,128)...) fusion(f32[4,4,2,128]{3,2,1,0:T(2,128)S(1)} %bitcast.421, ...), kind=kLoop, calls=%fused_computation.154.clone.1 | loop fusion | flops 26165248 | bytes 344064 | tf_op jit(solution)/shard_map/while/body/eval_jaxpr/vmap(vmap(vmap()))/reduce_sum | solution.py:69
  98.5 0.6 copy_dynamic-update-slice_fusion.4
  100.1 8.9 %fusion.142 = (f32[4,4,2,128]{3,2,1,0:T(2,128)S(1)}, f32[4,4,2,128]{3,2,1,0:T(2,128)S(1)}, f32[4,4,2,128]{3,2,1,0:T(2,128)S(1)}, f32[4,4,2,128]{3,2,1,0:T(2,128)...) fusion(f32[4,4,2,128]{3,2,1,0:T(2,128)S(1)} %bitcast.421, ...), kind=kLoop, calls=%fused_computation.154.clone.1 | loop fusion | flops 26165248 | bytes 344064 | tf_op jit(solution)/shard_map/while/body/eval_jaxpr/vmap(vmap(vmap()))/reduce_sum | solution.py:69
  109.4 0.6 copy_dynamic-update-slice_fusion.4
  111.0 8.9 %fusion.142 = (f32[4,4,2,128]{3,2,1,0:T(2,128)S(1)}, f32[4,4,2,128]{3,2,1,0:T(2,128)S(1)}, f32[4,4,2,128]{3,2,1,0:T(2,128)S(1)}, f32[4,4,2,128]{3,2,1,0:T(2,128)...) fusion(f32[4,4,2,128]{3,2,1,0:T(2,128)S(1)} %bitcast.421, ...), kind=kLoop, calls=%fused_computation.154.clone.1 | loop fusion | flops 26165248 | bytes 344064 | tf_op jit(solution)/shard_map/while/body/eval_jaxpr/vmap(vmap(vmap()))/reduce_sum | solution.py:69
  120.3 0.6 copy_dynamic-update-slice_fusion.4
  121.9 8.9 %fusion.142 = (f32[4,4,2,128]{3,2,1,0:T(2,128)S(1)}, f32[4,4,2,128]{3,2,1,0:T(2,128)S(1)}, f32[4,4,2,128]{3,2,1,0:T(2,128)S(1)}, f32[4,4,2,128]{3,2,1,0:T(2,128)...) fusion(f32[4,4,2,128]{3,2,1,0:T(2,128)S(1)} %bitcast.421, ...), kind=kLoop, calls=%fused_computation.154.clone.1 | loop fusion | flops 26165248 | bytes 344064 | tf_op jit(solution)/shard_map/while/body/eval_jaxpr/vmap(vmap(vmap()))/reduce_sum | solution.py:69
  131.2 0.6 copy_dynamic-update-slice_fusion.4
  131.8 3.4 %all-to-all-start.2 = ((f32[16,4,9,128]{3,1,2,0:T(4,128)}), f32[16,4,9,128]{3,1,2,0:T(4,128)S(1)}, u32[]{:S(2)}, u32[]{:S(2)}) async-start(f32[16,4,9,128]{3,1,2,0:T(4,128)} %bitcast.101), calls=%async_computation.2 | async-start | bytes 589824 | tf_op jit(solution)/shard_map/all_to_all | solution.py:104
  135.3 11.6 %while.53 = (s32[]{:T(128)}, f32[4,4,9,128]{3,1,0,2:T(4,128)S(1)}, f32[4,4,7,128]{3,1,0,2:T(4,128)S(1)}, f32[3,512]{1,0:T(4,128)S(1)}, f32[3,512]{1,0:T(4,128)S(1)}, /*index=5*/s32[]{:T(128)}) while((s32[]{:T(128)}, f32[4,4,9,128]{3,1,0,2:T(4,128)S(1)}, f32[4,4,7,128]{3,1,0,2:T(4,128)S(1)}, f32[3,512]{1,0:T(4,128)S(1)}, ...), condition=%wide.region_28.29_spmd, body=%wide.region_15.28_spmd.sunk | while | flops 12590593 | bytes 200781 | solution.py:151
  135.4 2.7 %fusion.144 = (f32[4,128]{1,0:T(4,128)S(1)}, f32[4,128]{1,0:T(4,128)S(1)}, f32[4,128]{1,0:T(4,128)S(1)}, f32[4,128]{1,0:T(4,128)S(1)}, f32[4,128]{1,0:T(4,128)S(...) fusion(f32[512]{0:T(512)S(1)} %bitcast.444, ...), kind=kLoop, calls=%fused_computation.36.clone.1 | loop fusion | flops 12576768 | bytes 45056 | tf_op jit(solution)/shard_map/while/body/eval_jaxpr/vmap()/reduce_sum | solution.py:69
  138.2 2.7 %fusion.144 = (f32[4,128]{1,0:T(4,128)S(1)}, f32[4,128]{1,0:T(4,128)S(1)}, f32[4,128]{1,0:T(4,128)S(1)}, f32[4,128]{1,0:T(4,128)S(1)}, f32[4,128]{1,0:T(4,128)S(...) fusion(f32[512]{0:T(512)S(1)} %bitcast.444, ...), kind=kLoop, calls=%fused_computation.36.clone.1 | loop fusion | flops 12576768 | bytes 45056 | tf_op jit(solution)/shard_map/while/body/eval_jaxpr/vmap()/reduce_sum | solution.py:69
  141.1 2.7 %fusion.144 = (f32[4,128]{1,0:T(4,128)S(1)}, f32[4,128]{1,0:T(4,128)S(1)}, f32[4,128]{1,0:T(4,128)S(1)}, f32[4,128]{1,0:T(4,128)S(1)}, f32[4,128]{1,0:T(4,128)S(...) fusion(f32[512]{0:T(512)S(1)} %bitcast.444, ...), kind=kLoop, calls=%fused_computation.36.clone.1 | loop fusion | flops 12576768 | bytes 45056 | tf_op jit(solution)/shard_map/while/body/eval_jaxpr/vmap()/reduce_sum | solution.py:69
  144.0 2.7 %fusion.144 = (f32[4,128]{1,0:T(4,128)S(1)}, f32[4,128]{1,0:T(4,128)S(1)}, f32[4,128]{1,0:T(4,128)S(1)}, f32[4,128]{1,0:T(4,128)S(1)}, f32[4,128]{1,0:T(4,128)S(...) fusion(f32[512]{0:T(512)S(1)} %bitcast.444, ...), kind=kLoop, calls=%fused_computation.36.clone.1 | loop fusion | flops 12576768 | bytes 45056 | tf_op jit(solution)/shard_map/while/body/eval_jaxpr/vmap()/reduce_sum | solution.py:69
  146.9 0.7 all-to-all-done.2
  148.1 0.6 add_bitcast_fusion
  149.0 0.7 broadcast_in_dim.57
  149.6 3.2 %all-to-all-start.8 = ((f32[4,3,2]{1,2,0:T(2,128)}), f32[4,3,2]{1,2,0:T(2,128)S(1)}, u32[]{:S(2)}, u32[]{:S(2)}) async-start(f32[4,3,2]{1,2,0:T(2,128)} %broadcast_in_dim.57), calls=%async_computation.8 | async-start | bytes 8192 | tf_op jit(solution)/shard_map/all_to_all | solution.py:25
  152.9 4.3 %all-to-all-done.8 = f32[4,3,2]{1,2,0:T(2,128)S(1)} async-done(((f32[4,3,2]{1,2,0:T(2,128)}), f32[4,3,2]{1,2,0:T(2,128)S(1)}, u32[]{:S(2)}, u32[]{:S(2)}) %all-to-all-start.8) | async-done | bytes 128 | tf_op jit(solution)/shard_map/all_to_all | solution.py:25
  157.3 0.7 broadcast_in_dim.58
  158.0 9.4 %all-to-all-start.9 = ((f32[64,4,3,2]{1,3,2,0:T(2,128)}), f32[64,4,3,2]{1,3,2,0:T(2,128)S(1)}, u32[]{:S(2)}, u32[]{:S(2)}) async-start(f32[64,4,3,2]{1,3,2,0:T(2,128)} %broadcast_in_dim.58), calls=%async_computation.9 | async-start | bytes 393216 | tf_op jit(solution)/shard_map/all_to_all | solution.py:25
  167.5 0.7 broadcast.958.clone
  168.2 43.6 %while.54 = (s32[]{:T(128)}, f32[4,4,4,9,128]{4,2,3,1,0:T(4,128)}, f32[4,4,4,3,128]{4,2,1,3,0:T(4,128)S(1)}, s32[4,4,4,2]{2,1,3,0:T(4,128)S(1)}, f32[16,7,128]{2...) while((s32[]{:T(128)}, f32[4,4,4,9,128]{4,2,3,1,0:T(4,128)}, ...), condition=%wide.region_43.44_spmd, body=%wide.region_29.43_spmd.sunk | while | flops 26289248 | bytes 1685093 | solution.py:100
  169.2 8.9 %fusion.147 = (f32[4,4,2,128]{3,2,1,0:T(2,128)S(1)}, f32[4,4,2,128]{3,2,1,0:T(2,128)S(1)}, f32[4,4,2,128]{3,2,1,0:T(2,128)S(1)}, f32[4,4,2,128]{3,2,1,0:T(2,128)...) fusion(f32[4,4,2,128]{3,2,1,0:T(2,128)S(1)} %bitcast.428, ...), kind=kLoop, calls=%fused_computation.213.clone.1 | loop fusion | flops 26165248 | bytes 344064 | tf_op jit(solution)/shard_map/while/body/eval_jaxpr/vmap(vmap(vmap()))/reduce_sum | solution.py:69
  178.5 0.6 copy_dynamic-update-slice_fusion.5
  180.1 8.9 %fusion.147 = (f32[4,4,2,128]{3,2,1,0:T(2,128)S(1)}, f32[4,4,2,128]{3,2,1,0:T(2,128)S(1)}, f32[4,4,2,128]{3,2,1,0:T(2,128)S(1)}, f32[4,4,2,128]{3,2,1,0:T(2,128)...) fusion(f32[4,4,2,128]{3,2,1,0:T(2,128)S(1)} %bitcast.428, ...), kind=kLoop, calls=%fused_computation.213.clone.1 | loop fusion | flops 26165248 | bytes 344064 | tf_op jit(solution)/shard_map/while/body/eval_jaxpr/vmap(vmap(vmap()))/reduce_sum | solution.py:69
  189.4 0.6 copy_dynamic-update-slice_fusion.5
  190.2 0.6 gather_fusion.1
  191.0 8.9 %fusion.147 = (f32[4,4,2,128]{3,2,1,0:T(2,128)S(1)}, f32[4,4,2,128]{3,2,1,0:T(2,128)S(1)}, f32[4,4,2,128]{3,2,1,0:T(2,128)S(1)}, f32[4,4,2,128]{3,2,1,0:T(2,128)...) fusion(f32[4,4,2,128]{3,2,1,0:T(2,128)S(1)} %bitcast.428, ...), kind=kLoop, calls=%fused_computation.213.clone.1 | loop fusion | flops 26165248 | bytes 344064 | tf_op jit(solution)/shard_map/while/body/eval_jaxpr/vmap(vmap(vmap()))/reduce_sum | solution.py:69
  200.2 0.6 copy_dynamic-update-slice_fusion.5
  201.1 0.6 gather_fusion.1
  201.9 8.9 %fusion.147 = (f32[4,4,2,128]{3,2,1,0:T(2,128)S(1)}, f32[4,4,2,128]{3,2,1,0:T(2,128)S(1)}, f32[4,4,2,128]{3,2,1,0:T(2,128)S(1)}, f32[4,4,2,128]{3,2,1,0:T(2,128)...) fusion(f32[4,4,2,128]{3,2,1,0:T(2,128)S(1)} %bitcast.428, ...), kind=kLoop, calls=%fused_computation.213.clone.1 | loop fusion | flops 26165248 | bytes 344064 | tf_op jit(solution)/shard_map/while/body/eval_jaxpr/vmap(vmap(vmap()))/reduce_sum | solution.py:69
  211.1 0.6 copy_dynamic-update-slice_fusion.5
  211.8 7.2 %all-to-all-start.7 = ((f32[16,4,9,128]{3,1,2,0:T(4,128)}), f32[16,4,9,128]{3,1,2,0:T(4,128)S(1)}, u32[]{:S(2)}, u32[]{:S(2)}) async-start(f32[16,4,9,128]{3,1,2,0:T(4,128)} %bitcast.114), calls=%async_computation.7 | async-start | bytes 589824 | tf_op jit(solution)/shard_map/all_to_all | solution.py:104
  219.7 11.6 %while.55 = (s32[]{:T(128)}, f32[4,4,9,128]{3,1,0,2:T(4,128)S(1)}, f32[4,4,7,128]{3,1,0,2:T(4,128)S(1)}, f32[3,512]{1,0:T(4,128)S(1)}, f32[3,512]{1,0:T(4,128)S(1)}, /*index=5*/s32[]{:T(128)}) while((s32[]{:T(128)}, f32[4,4,9,128]{3,1,0,2:T(4,128)S(1)}, f32[4,4,7,128]{3,1,0,2:T(4,128)S(1)}, f32[3,512]{1,0:T(4,128)S(1)}, ...), condition=%wide.region_57.58_spmd, body=%wide.region_44.57_spmd.sunk | while | flops 12590593 | bytes 200781 | solution.py:151
  219.8 2.7 %fusion.149 = (f32[4,128]{1,0:T(4,128)S(1)}, f32[4,128]{1,0:T(4,128)S(1)}, f32[4,128]{1,0:T(4,128)S(1)}, f32[4,128]{1,0:T(4,128)S(1)}, f32[4,128]{1,0:T(4,128)S(...) fusion(f32[512]{0:T(512)S(1)} %bitcast.450, ...), kind=kLoop, calls=%fused_computation.95.clone.1 | loop fusion | flops 12576768 | bytes 45056 | tf_op jit(solution)/shard_map/while/body/eval_jaxpr/vmap()/reduce_sum | solution.py:69
  222.7 2.7 %fusion.149 = (f32[4,128]{1,0:T(4,128)S(1)}, f32[4,128]{1,0:T(4,128)S(1)}, f32[4,128]{1,0:T(4,128)S(1)}, f32[4,128]{1,0:T(4,128)S(1)}, f32[4,128]{1,0:T(4,128)S(...) fusion(f32[512]{0:T(512)S(1)} %bitcast.450, ...), kind=kLoop, calls=%fused_computation.95.clone.1 | loop fusion | flops 12576768 | bytes 45056 | tf_op jit(solution)/shard_map/while/body/eval_jaxpr/vmap()/reduce_sum | solution.py:69
  225.6 2.7 %fusion.149 = (f32[4,128]{1,0:T(4,128)S(1)}, f32[4,128]{1,0:T(4,128)S(1)}, f32[4,128]{1,0:T(4,128)S(1)}, f32[4,128]{1,0:T(4,128)S(1)}, f32[4,128]{1,0:T(4,128)S(...) fusion(f32[512]{0:T(512)S(1)} %bitcast.450, ...), kind=kLoop, calls=%fused_computation.95.clone.1 | loop fusion | flops 12576768 | bytes 45056 | tf_op jit(solution)/shard_map/while/body/eval_jaxpr/vmap()/reduce_sum | solution.py:69
  228.5 2.7 %fusion.149 = (f32[4,128]{1,0:T(4,128)S(1)}, f32[4,128]{1,0:T(4,128)S(1)}, f32[4,128]{1,0:T(4,128)S(1)}, f32[4,128]{1,0:T(4,128)S(1)}, f32[4,128]{1,0:T(4,128)S(...) fusion(f32[512]{0:T(512)S(1)} %bitcast.450, ...), kind=kLoop, calls=%fused_computation.95.clone.1 | loop fusion | flops 12576768 | bytes 45056 | tf_op jit(solution)/shard_map/while/body/eval_jaxpr/vmap()/reduce_sum | solution.py:69
  231.9 0.6 copy.299
  (315 shorter events, 14.4 us)
Async XLA Ops:
  0.6 7.9 %copy-start.2 = (s32[16,4]{0,1:T(4,128)S(1)}, s32[16,4]{0,1:T(4,128)}, u32[]{:S(2)}) copy-start(s32[16,4]{0,1:T(4,128)} %param.21) | copy-start | bytes 772
  0.6 7.9 %copy-start.3 = (s32[64,2]{0,1:T(2,128)S(1)}, s32[64,2]{0,1:T(2,128)}, u32[]{:S(2)}) copy-start(s32[64,2]{0,1:T(2,128)} %param.22) | copy-start | bytes 1540
  0.7 12.0 %copy-start.4 = (f32[3,2]{0,1:T(2,128)S(1)}, f32[3,2]{0,1:T(2,128)}, u32[]{:S(2)}) copy-start(f32[3,2]{0,1:T(2,128)} %param.20) | copy-start | bytes 76
  0.7 31.7 %copy-start.5 = (s32[16]{0:T(128)S(1)}, s32[16]{0:T(128)}, u32[]{:S(2)}) copy-start(s32[16]{0:T(128)} %param.23) | copy-start | bytes 196
  3.7 9.0 %all-to-all-start.5 = ((f32[4,3,2]{1,2,0:T(2,128)}), f32[4,3,2]{1,2,0:T(2,128)S(1)}, u32[]{:S(2)}, u32[]{:S(2)}) async-start(f32[4,3,2]{1,2,0:T(2,128)} %broadcast_in_dim.55), calls=%async_computation.5 | async-start | bytes 8192 | tf_op jit(solution)/shard_map/all_to_all | solution.py:25
  13.2 7.4 %all-to-all-start.3 = ((f32[4,3,2]{1,2,0:T(2,128)}), f32[4,3,2]{1,2,0:T(2,128)S(1)}, u32[]{:S(2)}, u32[]{:S(2)}) async-start(f32[4,3,2]{1,2,0:T(2,128)} %broadcast_in_dim.53), calls=%async_computation.3 | async-start | bytes 8192 | tf_op jit(solution)/shard_map/all_to_all | solution.py:25
  20.6 19.1 %all-to-all-start.1 = ((s32[16,4,2]{1,2,0:T(2,128)}), s32[16,4,2]{1,2,0:T(2,128)S(1)}, u32[]{:S(2)}, u32[]{:S(2)}) async-start(s32[16,4,2]{1,2,0:T(2,128)} %copy.233), calls=%async_computation.1 | async-start | bytes 32768 | tf_op jit(solution)/shard_map/all_to_all | solution.py:120
  40.4 16.5 %all-to-all-start.6 = ((f32[64,4,3,2]{1,3,2,0:T(2,128)}), f32[64,4,3,2]{1,3,2,0:T(2,128)S(1)}, u32[]{:S(2)}, u32[]{:S(2)}) async-start(f32[64,4,3,2]{1,3,2,0:T(2,128)} %broadcast_in_dim.56), calls=%async_computation.6 | async-start | bytes 393216 | tf_op jit(solution)/shard_map/all_to_all | solution.py:25
  57.6 16.6 %all-to-all-start.4 = ((f32[64,4,3,2]{1,3,2,0:T(2,128)}), f32[64,4,3,2]{1,3,2,0:T(2,128)S(1)}, u32[]{:S(2)}, u32[]{:S(2)}) async-start(f32[64,4,3,2]{1,3,2,0:T(2,128)} %broadcast_in_dim.54), calls=%async_computation.4 | async-start | bytes 393216 | tf_op jit(solution)/shard_map/all_to_all | solution.py:25
  74.2 13.1 %all-to-all-start = ((f32[16,4,4,128]{3,2,1,0:T(4,128)}), f32[16,4,4,128]{3,2,1,0:T(4,128)S(1)}, u32[]{:S(2)}, u32[]{:S(2)}) async-start(f32[16,4,4,128]{3,2,1,0:T(4,128)} %pad_maximum_fusion), calls=%async_computation | async-start | bytes 262144 | tf_op jit(solution)/shard_map/all_to_all | solution.py:119
  131.8 15.8 %all-to-all-start.2 = ((f32[16,4,9,128]{3,1,2,0:T(4,128)}), f32[16,4,9,128]{3,1,2,0:T(4,128)S(1)}, u32[]{:S(2)}, u32[]{:S(2)}) async-start(f32[16,4,9,128]{3,1,2,0:T(4,128)} %bitcast.101), calls=%async_computation.2 | async-start | bytes 589824 | tf_op jit(solution)/shard_map/all_to_all | solution.py:104
  146.9 1.3 copy-start
  147.6 1.2 copy-start.1
  148.1 0.7 copy-start.6
  149.6 7.6 %all-to-all-start.8 = ((f32[4,3,2]{1,2,0:T(2,128)}), f32[4,3,2]{1,2,0:T(2,128)S(1)}, u32[]{:S(2)}, u32[]{:S(2)}) async-start(f32[4,3,2]{1,2,0:T(2,128)} %broadcast_in_dim.57), calls=%async_computation.8 | async-start | bytes 8192 | tf_op jit(solution)/shard_map/all_to_all | solution.py:25
  158.0 53.8 %all-to-all-start.9 = ((f32[64,4,3,2]{1,3,2,0:T(2,128)}), f32[64,4,3,2]{1,3,2,0:T(2,128)S(1)}, u32[]{:S(2)}, u32[]{:S(2)}) async-start(f32[64,4,3,2]{1,3,2,0:T(2,128)} %broadcast_in_dim.58), calls=%async_computation.9 | async-start | bytes 393216 | tf_op jit(solution)/shard_map/all_to_all | solution.py:25
  211.8 19.5 %all-to-all-start.7 = ((f32[16,4,9,128]{3,1,2,0:T(4,128)}), f32[16,4,9,128]{3,1,2,0:T(4,128)S(1)}, u32[]{:S(2)}, u32[]{:S(2)}) async-start(f32[16,4,9,128]{3,1,2,0:T(4,128)} %bitcast.114), calls=%async_computation.7 | async-start | bytes 589824 | tf_op jit(solution)/shard_map/all_to_all | solution.py:104
where the time goes:
time: 233 us; the launch traced here: 232 us
  other arithmetic  99.2 us (43%)
  starting transfers between devices  58.6 us (25%)
  waiting for transfers between devices  47.4 us (20%)
  local copies, waits for them, and re-layouts  23 us (10%)
    reduce_sum x16, other arithmetic, tile_gradient(): term = jnp.sum(weighted * dists[second], axis=1)  92.3 us
    all_to_all x6, waiting for transfers between devices, from_everyone(): lax.all_to_all(jnp.broadcast_to(shard[None], (peers, *shard.shape)), axis...  32.2 us
    all_to_all x6, starting transfers between devices, from_everyone(): lax.all_to_all(jnp.broadcast_to(shard[None], (peers, *shard.shape)), axis...  32 us
    all_to_all x1, starting transfers between devices, evaluate(): lax.all_to_all(pair_rows, GY, split_axis=0, concat_axis=0, tiled=True)  11.7 us
    all_to_all x2, starting transfers between devices, send_back(): lax.all_to_all(partial_terms, GY, split_axis=0, concat_axis=0, tiled=True)  10.7 us
    all_to_all x1, waiting for transfers between devices, evaluate(): lax.all_to_all(payload, GY, split_axis=0, concat_axis=0, tiled=True)  7.48 us
    all_to_all x1, waiting for transfers between devices, evaluate(): lax.all_to_all(pair_rows, GY, split_axis=0, concat_axis=0, tiled=True)  7.05 us
    dynamic_update_slice x8, local copies, waits for them, and re-layouts, remote_terms(): return lax.map(per_peer, (tpos, tcore, None, rows), batch_size=4)  5.14 us
  transfers between devices with their start and end apart: 10, of which 8 were waited for; matrix products, arithmetic and copies ran while one was open for 31% of the time, Pallas kernels for 0%

commit v1 on v0

v1 whole, which is shorter than its diff:
```python
import functools
import math

import jax
import jax.numpy as jnp
from jax import lax
from jax.experimental import pallas as pl
from jax.experimental.pallas import tpu as pltpu
from jax.sharding import PartitionSpec as P

BLOCK = 128
NB = 16
SLOTS = 4
GX_GY = ("gx", "gy")
F32 = jnp.float32
BF16 = jnp.bfloat16

far_core = 1.0
step_size = 0.1
inv_four_pi = 1.0 / (4.0 * math.pi)

PEERS = 16
CHIPS = 8
NEAR = PEERS * SLOTS
UNITS = NEAR + 2 * NB
SRC = PEERS * NB


def dot_t(left, right):
    return lax.dot_general(left, right, (((1,), (1,)), ((), ())), preferred_element_type=F32)


def rounded(value):
    return value.astype(BF16).astype(F32)


def kernel(
    pos, strg, cor, cell, cen, sb, pr, cnt,
    out1, out2,
    land, land2, gxa, gya, gxb, gyb,
    tb, ta, sp, ab, w, pb, k5, rm, rk, nm, nk,
    ring_s, ring_r, ring2_s, ring2_r, gxs, gxr, gys, gyr, gxs2, gxr2, gys2, gyr2,
):
    gx, gy = lax.axis_index("gx"), lax.axis_index("gy")
    z, c = gy // 2, gy % 2
    sgn = 1 - 2 * c

    def chip(offset):
        return (z + offset + CHIPS) % CHIPS

    barrier = pltpu.get_barrier_semaphore()

    @pl.loop(1, PEERS)
    def _(d):
        pl.semaphore_signal(
            barrier, inc=1, device_id={"gx": (gx + d) % PEERS},
            device_id_type=pl.DeviceIdType.MESH)
        pl.semaphore_signal(
            barrier, inc=1, device_id={"gy": (gy + d) % PEERS},
            device_id_type=pl.DeviceIdType.MESH)

    for b in range(NB):
        cols = slice(b * BLOCK, (b + 1) * BLOCK)
        for r in range(3):
            land[gy, r, b : b + 1, :] = pos[r : r + 1, cols]
            land[gy, 3 + r, b : b + 1, :] = strg[r : r + 1, cols]
    land[gy, 6] = 0.5 * cor[...] * cor[...]

    rows8 = lax.broadcasted_iota(jnp.int32, (8, BLOCK), 0)
    lanes8 = lax.broadcasted_iota(jnp.int32, (8, BLOCK), 1)
    my_lane = 32 * (gy % 4) + 2 * gx

    def cell_tile(comps, centers):
        tile = jnp.zeros((8, BLOCK), F32)
        for one in range(2):
            here = lanes8 == my_lane + one
            chosen = (cell[...] == one).astype(F32)
            for r in range(3):
                total = jnp.sum(comps[r] * chosen, axis=(0, 1), keepdims=True)
                tile = jnp.where(here & (rows8 == r), total, tile)
                if centers:
                    tile = jnp.where(here & (rows8 == 3 + r), cen[r, one], tile)
        return tile

    gxa[gx] = cell_tile([land[gy, 3 + r] for r in range(3)], True)

    def remote(src, dst, ss, rs, where):
        return pltpu.make_async_remote_copy(
            src_ref=src, dst_ref=dst, send_sem=ss, recv_sem=rs,
            device_id=where, device_id_type=pl.DeviceIdType.MESH)

    def spread(buf, me, axis, ss, rs):
        @pl.loop(1, PEERS)
        def _(d):
            remote(buf.at[me], buf.at[me], ss.at[d], rs.at[d], {axis: (me + d) % PEERS}).start()

    def spread_recv(buf, me, axis, ss, rs):
        @pl.loop(1, PEERS)
        def _(d):
            of = (me - d + PEERS) % PEERS
            remote(buf.at[of], buf.at[of], ss.at[d], rs.at[d], {axis: (me + d) % PEERS}).wait_recv()

    def spread_sent(buf, me, axis, ss, rs):
        @pl.loop(1, PEERS)
        def _(d):
            remote(buf.at[me], buf.at[me], ss.at[d], rs.at[d], {axis: (me + d) % PEERS}).wait_send()

    sibling = z * 2 + 1 - c

    def ring_a(buf, s, ss, rs):
        owner = chip(-(s - 1) * sgn) * 2 + c
        return remote(buf.at[owner], buf.at[owner], ss.at[s - 1], rs.at[s - 1],
                      {"gy": chip(sgn) * 2 + c})

    def ring_b(buf, s, ss, rs):
        owner = chip((s - 1) * sgn) * 2 + c
        return remote(buf.at[owner], buf.at[owner], ss.at[3 + s], rs.at[3 + s],
                      {"gy": chip(-sgn) * 2 + c})

    def across(buf, j, ss, rs):
        off = 0 if j == 0 else (-j * sgn if j <= 4 else (j - 4) * sgn)
        owner = chip(off) * 2 + c
        return remote(buf.at[owner], buf.at[owner], ss.at[7 + j], rs.at[7 + j], {"gy": sibling})

    def ring_a_recv(buf, s, ss, rs):
        owner = chip(-s * sgn) * 2 + c
        remote(buf.at[owner], buf.at[owner], ss.at[s - 1], rs.at[s - 1],
               {"gy": chip(sgn) * 2 + c}).wait_recv()

    def ring_b_recv(buf, s, ss, rs):
        owner = chip(s * sgn) * 2 + c
        remote(buf.at[owner], buf.at[owner], ss.at[3 + s], rs.at[3 + s],
               {"gy": chip(-sgn) * 2 + c}).wait_recv()

    def across_recv(buf, j, ss, rs):
        off = 0 if j == 0 else (j * sgn if j <= 4 else -(j - 4) * sgn)
        owner = chip(off) * 2 + 1 - c
        remote(buf.at[owner], buf.at[owner], ss.at[7 + j], rs.at[7 + j],
               {"gy": sibling}).wait_recv()

    def ring_start(buf, ss, rs):
        ring_a(buf, 1, ss, rs).start()
        ring_b(buf, 1, ss, rs).start()
        across(buf, 0, ss, rs).start()

    def ring_step(buf, s, ss, rs):
        ring_a_recv(buf, s, ss, rs)
        if s < 4:
            ring_a(buf, s + 1, ss, rs).start()
        across(buf, s, ss, rs).start()
        if s < 4:
            ring_b_recv(buf, s, ss, rs)
            if s < 3:
                ring_b(buf, s + 1, ss, rs).start()
            across(buf, 4 + s, ss, rs).start()

    def ring_sent(buf, ss, rs):
        for s in range(1, 5):
            ring_a(buf, s, ss, rs).wait_send()
            if s < 4:
                ring_b(buf, s, ss, rs).wait_send()
        for j in range(8):
            across(buf, j, ss, rs).wait_send()

    def columns(p, a, base, count):
        b0 = p[1] * a[2] - p[2] * a[1]
        b1 = p[2] * a[0] - p[0] * a[2]
        b2 = p[0] * a[1] - p[1] * a[0]
        for r, value in enumerate([a[0], a[1], a[2], b0, b1, b2]):
            ab[pl.ds(r, count, stride=8), :] = value
        pieces(base, count)

    def pieces(base, count):
        full = ab[0 : count * 8, :]
        hi = rounded(full)
        rest = full - hi
        mid = rounded(rest)
        low = rest - mid
        nothing = jnp.zeros((8, BLOCK), F32)
        for b in range(count):
            part = slice(b * 8, b * 8 + 8)
            both = jnp.concatenate([hi[part], mid[part]], axis=0)
            w[base + b, 0:16, :] = both.astype(BF16)
            w[base + b, 16:32, :] = jnp.concatenate([low[part], nothing], axis=0).astype(BF16)

    def prep(g):
        p = [land[g, r] for r in range(3)]
        for r, value in enumerate(p + [land[g, 6]]):
            ab[pl.ds(r, NB, stride=8), :] = value
        for b in range(NB):
            sp[g * NB + b] = ab[b * 8 : b * 8 + 8, :]
        columns(p, [land[g, 3 + r] for r in range(3)], g * NB, NB)

    def prep_again(g):
        columns([land[g, r] for r in range(3)], [land2[g, r] for r in range(3)], g * NB, NB)

    def source_rows(s):
        return sp[s]

    def halves(value):
        hi = value.astype(BF16)
        return hi, (value - hi.astype(F32)).astype(BF16)

    def tile_first(u, t, s0, s1):
        tiles = [source_rows(s0), source_rows(s1)]
        spread_rows = [
            [jnp.broadcast_to(tile[r : r + 1, :], (16, BLOCK)) for r in range(4)] for tile in tiles
        ]
        for i in range(8):
            rows = pl.ds(i * 16, 16)
            tx, ty, tz, tc = (tb[t, r, rows, :] for r in range(4))
            ax, ay, az = (ta[t, r, rows, :] for r in range(3))
            for h in range(2):
                cols = slice(h * BLOCK, (h + 1) * BLOCK)
                sx, sy, sz, sc = spread_rows[h]
                rx, ry, rz = tx - sx, ty - sy, tz - sz
                q = (rx * rx + ry * ry) + (rz * rz + (tc + sc))
                inv = lax.rsqrt(q)
                inv2 = inv * inv
                k3 = inv2 * inv
                five = k3 * inv2
                k5[u, rows, cols] = five
                m = five * (rx * ax + ry * ay + rz * az)
                for j, piece in enumerate([*halves(m), *halves(k3)]):
                    pb[u, pl.ds(j * BLOCK + i * 16, 16), cols] = piece

    def tile_second(u, t, s0, s1):
        tiles = [source_rows(s0), source_rows(s1)]
        spread_rows = [
            [jnp.broadcast_to(tile[r : r + 1, :], (16, BLOCK)) for r in range(3)] for tile in tiles
        ]
        for i in range(8):
            rows = pl.ds(i * 16, 16)
            tx, ty, tz = (tb[t, r, rows, :] for r in range(3))
            ax, ay, az = (ta[t, r, rows, :] for r in range(3))
            for h in range(2):
                cols = slice(h * BLOCK, (h + 1) * BLOCK)
                sx, sy, sz = spread_rows[h]
                rx, ry, rz = tx - sx, ty - sy, tz - sz
                m = k5[u, rows, cols] * (rx * ax + ry * ay + rz * az)
                for j, piece in enumerate(halves(m)):
                    pb[u, pl.ds(j * BLOCK + i * 16, 16), cols] = piece

    def source_columns(s):
        return w[s]

    def near_products(u):
        g = u // SLOTS
        products(u, g * NB + pr[u, 0], g * NB + pr[u, 1])

    def far_products(u):
        half = u % 2
        products(u, SRC + 2 * half, SRC + 2 * half + 1)

    def products(u, s0, s1):
        left = jnp.concatenate([source_columns(s0), source_columns(s1)], axis=1)
        got = dot_t(left, pb[u])

        def folded(first):
            part = got[:, first : first + BLOCK] + got[:, first + BLOCK : first + 2 * BLOCK]
            return part[0:8] + part[8:16] + part[16:24]

        rm[u] = folded(0)
        rk[u] = folded(2 * BLOCK)

    def near_unit(g, k):
        u = g * SLOTS + k
        return u, sb[g, k], g * NB + pr[u, 0], g * NB + pr[u, 1]

    def far_unit(index):
        t, half = index // 2, index % 2
        return NEAR + index, t, SRC + 2 * half, SRC + 2 * half + 1

    def first_pass(unit_of, count, before, finish_one=near_products):
        def body(index, carry):
            finish_one(carry)
            u, t, s0, s1 = unit_of(index)
            tile_first(u, t, s0, s1)
            return u

        return lax.fori_loop(0, count, body, before)

    def near_units(owner_of):
        return lambda index: near_unit(owner_of(index // SLOTS), index % SLOTS)

    def prep_all(owner_of, count, how):
        @pl.loop(0, count)
        def _(j):
            how(owner_of(j))

    def mine_at(s):
        return lambda j: chip((2 * j - 1) * s * sgn) * 2 + c

    def theirs_at(s):
        return lambda j: chip((1 - 2 * j) * s * sgn) * 2 + 1 - c

    def far_rows(buf):
        tiles = []
        for four in range(4):
            total = buf[4 * four]
            for one in range(1, 4):
                total = total + buf[4 * four + one]
            own = (four == gy // 4) & ((lanes8 == my_lane) | (lanes8 == my_lane + 1))
            tiles.append(jnp.where(own & (rows8 < 3), 0.0, total))
        return tiles

    def summed(buf):
        total = buf[0]
        for one in range(1, PEERS):
            total = total + buf[one]
        return total

    def far_columns(tiles, centers):
        for four, tile in enumerate(tiles):
            p = [centers[four][3 + r : 4 + r, :] for r in range(3)]
            a = [tile[r : r + 1, :] for r in range(3)]
            b0 = p[1] * a[2] - p[2] * a[1]
            b1 = p[2] * a[0] - p[0] * a[2]
            b2 = p[0] * a[1] - p[1] * a[0]
            for r, value in enumerate([a[0], a[1], a[2], b0, b1, b2]):
                ab[four * 8 + r : four * 8 + r + 1, :] = value
        pieces(SRC, 4)

    def broadcast_targets(ref, rows_of):
        @pl.loop(0, NB)
        def _(t):
            for r, row in enumerate(rows_of):
                line = row(t)
                ref[t, r] = jnp.broadcast_to(line, (BLOCK, BLOCK)).T

    def land_row(r):
        return lambda t: land[gy, r, pl.ds(t, 1), :]

    broadcast_targets(tb, [land_row(r) for r in (0, 1, 2, 6)])
    broadcast_targets(ta, [land_row(r) for r in (3, 4, 5)])
    ab[...] = jnp.zeros_like(ab)

    lane_u = lax.broadcasted_iota(jnp.int32, (8, UNITS * 8), 1)
    unit_u = lane_u // 8
    row_u = lax.broadcasted_iota(jnp.int32, (8, UNITS * 8), 0)
    fed = jnp.where(unit_u >= NEAR, (unit_u - NEAR) // 2, -1)
    live = jnp.ones_like(fed)
    for g in range(PEERS):
        for k in range(SLOTS):
            here = unit_u == g * SLOTS + k
            fed = jnp.where(here, sb[g, k], fed)
            live = jnp.where(here, cnt[g] - k, live)
    same = (lane_u % 8 == row_u) & (live > 0)
    select = jnp.concatenate(
        [jnp.where(same & (fed == t), 1.0, 0.0).astype(F32) for t in range(NB)], axis=0
    ).astype(BF16)

    pl.semaphore_wait(barrier, 2 * (PEERS - 1))

    ring_start(land, ring_s, ring_r)
    spread(gxa, gx, "gx", gxs, gxr)

    prep(gy)
    u, t, s0, s1 = near_unit(gy, 0)
    tile_first(u, t, s0, s1)
    carry = u
    carry = first_pass(lambda index: near_unit(gy, index + 1), 3, carry)

    spread_recv(gxa, gx, "gx", gxs, gxr)
    gya[gy] = summed(gxa)
    spread(gya, gy, "gy", gys, gyr)

    across_recv(land, 0, ring_s, ring_r)
    prep(sibling)
    carry = first_pass(lambda index: near_unit(sibling, index), SLOTS, carry)
    for s in range(1, 5):
        ring_step(land, s, ring_s, ring_r)
        count = 2 if s < 4 else 1
        prep_all(mine_at(s), count, prep)
        carry = first_pass(near_units(mine_at(s)), count * SLOTS, carry)
        across_recv(land, s, ring_s, ring_r)
        if s < 4:
            across_recv(land, 4 + s, ring_s, ring_r)
        prep_all(theirs_at(s), count, prep)
        carry = first_pass(near_units(theirs_at(s)), count * SLOTS, carry)

    spread_recv(gya, gy, "gy", gys, gyr)
    centers = far_rows(gya)
    for four in range(4):
        for r in range(3):
            sp[SRC + four, r : r + 1, :] = centers[four][3 + r : 4 + r, :]
        sp[SRC + four, 3:4, :] = jnp.full((1, BLOCK), 0.5 * far_core * far_core, F32)
    far_columns(centers, centers)
    near_products(carry)
    u, t, s0, s1 = far_unit(0)
    tile_first(u, t, s0, s1)
    carry = first_pass(lambda index: far_unit(index + 1), 2 * NB - 1, u, far_products)
    far_products(carry)

    def finish(a, p, out):
        for many, one in ((rm, nm), (rk, nk)):
            full = many[...].reshape(UNITS * 8, BLOCK)
            hi = full.astype(BF16)
            rest = full - hi.astype(F32)
            mid = rest.astype(BF16)
            low = (rest - mid.astype(F32)).astype(BF16)
            one[...] = (
                jnp.dot(select, hi, preferred_element_type=F32)
                + jnp.dot(select, mid, preferred_element_type=F32)
                + jnp.dot(select, low, preferred_element_type=F32)
            )
        sa = [nm[pl.ds(r, NB, stride=8), :] for r in range(3)]
        sq = [nm[pl.ds(3 + r, NB, stride=8), :] for r in range(3)]
        sk = [nk[pl.ds(r, NB, stride=8), :] for r in range(3)]
        result = []
        for r in range(3):
            i, j = (r + 1) % 3, (r + 2) % 3
            turned = p[i] * sa[j] - p[j] * sa[i] - sq[r]
            twisted = a[i] * sk[j] - a[j] * sk[i]
            result.append((3.0 * turned - twisted) * inv_four_pi)
        for r in range(3):
            for b in range(NB):
                out[r : r + 1, b * BLOCK : (b + 1) * BLOCK] = result[r][b : b + 1, :]
        return result

    first = finish([land[gy, 3 + r] for r in range(3)], [land[gy, r] for r in range(3)], out1)

    for r in range(3):
        land2[gy, r] = land[gy, 3 + r] + step_size * first[r]
    moved = [land2[gy, r] for r in range(3)]
    gxb[gx] = cell_tile(moved, False)
    spread(gxb, gx, "gx", gxs2, gxr2)
    ring_start(land2, ring2_s, ring2_r)

    broadcast_targets(ta, [(lambda t, r=r: land2[gy, r, pl.ds(t, 1), :]) for r in range(3)])
    spread_recv(gxb, gx, "gx", gxs2, gxr2)
    gyb[gy] = summed(gxb)
    spread(gyb, gy, "gy", gys2, gyr2)

    def second_tiles(unit_of, first_index, last_index):
        @pl.loop(first_index, last_index)
        def _(index):
            tile_second(*unit_of(index))

    by_slot = lambda index: near_unit(index // SLOTS, index % SLOTS)
    for s in range(1, 5):
        second_tiles(by_slot, (s - 1) * 16, s * 16)
        ring_step(land2, s, ring2_s, ring2_r)
    second_tiles(far_unit, 0, 2 * NB)

    def second_products(g):
        prep_again(g)
        for k in range(SLOTS):
            u, t, s0, s1 = near_unit(g, k)
            products(u, s0, s1)

    for j in range(8):
        across_recv(land2, j, ring2_s, ring2_r)

    @pl.loop(0, PEERS)
    def _(g):
        second_products(g)

    spread_recv(gyb, gy, "gy", gys2, gyr2)
    far_columns(far_rows(gyb), centers)

    @pl.loop(0, NB // 2)
    def _(index):
        for one in range(4):
            u, t, s0, s1 = far_unit(index * 4 + one)
            products(u, s0, s1)

    finish(moved, [land[gy, r] for r in range(3)], out2)

    ring_sent(land, ring_s, ring_r)
    ring_sent(land2, ring2_s, ring2_r)
    spread_sent(gxa, gx, "gx", gxs, gxr)
    spread_sent(gya, gy, "gy", gys, gyr)
    spread_sent(gxb, gx, "gx", gxs2, gxr2)
    spread_sent(gyb, gy, "gy", gys2, gyr2)


def body(positions, strengths, cores, cell_local, cell_centers, send_blocks, pair_src, counts):
    vmem = pl.BlockSpec(memory_space=pltpu.VMEM)
    smem = pl.BlockSpec(memory_space=pltpu.SMEM)
    dma = pltpu.SemaphoreType.DMA
    shape = jax.ShapeDtypeStruct(positions.shape, F32)
    return pl.pallas_call(
        kernel,
        out_shape=(shape, shape),
        in_specs=[vmem] * 4 + [smem] * 4,
        out_specs=(vmem, vmem),
        scratch_shapes=[
            pltpu.VMEM((PEERS, 7, NB, BLOCK), F32),
            pltpu.VMEM((PEERS, 3, NB, BLOCK), F32),
            pltpu.VMEM((PEERS, 8, BLOCK), F32),
            pltpu.VMEM((PEERS, 8, BLOCK), F32),
            pltpu.VMEM((PEERS, 8, BLOCK), F32),
            pltpu.VMEM((PEERS, 8, BLOCK), F32),
            pltpu.VMEM((NB, 4, BLOCK, BLOCK), F32),
            pltpu.VMEM((NB, 3, BLOCK, BLOCK), F32),
            pltpu.VMEM((SRC + 4, 8, BLOCK), F32),
            pltpu.VMEM((NB * 8, BLOCK), F32),
            pltpu.VMEM((SRC + 4, 32, BLOCK), BF16),
            pltpu.VMEM((UNITS, 4 * BLOCK, 2 * BLOCK), BF16),
            pltpu.VMEM((UNITS, BLOCK, 2 * BLOCK), F32),
            pltpu.VMEM((UNITS, 8, BLOCK), F32),
            pltpu.VMEM((UNITS, 8, BLOCK), F32),
            pltpu.VMEM((NB * 8, BLOCK), F32),
            pltpu.VMEM((NB * 8, BLOCK), F32),
            dma((15,)), dma((15,)), dma((15,)), dma((15,)),
            dma((PEERS,)), dma((PEERS,)), dma((PEERS,)), dma((PEERS,)),
            dma((PEERS,)), dma((PEERS,)), dma((PEERS,)), dma((PEERS,)),
        ],
        compiler_params=pltpu.CompilerParams(
            collective_id=0, has_side_effects=True, vmem_limit_bytes=62 << 20),
        name="vortex",
    )(positions, strengths, cores.reshape(NB, BLOCK), cell_local.reshape(NB, BLOCK),
      cell_centers, send_blocks, pair_src, counts)


def solution(mesh):
    placed = (
        P(None, GX_GY), P(None, GX_GY), P(GX_GY), P(GX_GY),
        P(None, GX_GY), P(GX_GY, None), P(GX_GY, None), P(GX_GY),
    )
    return jax.shard_map(
        body, mesh=mesh, in_specs=placed,
        out_specs=(P(None, GX_GY), P(None, GX_GY)), check_vma=False)
```

time: 233 us -> 74 us (0.32)
  other arithmetic: 99.2 us -> 0 us
  Pallas kernels: 0 us -> 68.3 us
  starting transfers between devices: 58.6 us -> 0 us
  waiting for transfers between devices: 47.4 us -> 0 us
  local copies, waits for them, and re-layouts: 23 us -> 4.74 us
    reduce_sum x24 -> x0, other arithmetic: 93.8 us -> none  [the longest x16 92.3 us: tile_gradient(): term = jnp.sum(weighted * dists[second], axis=1)]
    pallas_call x0 -> x1, Pallas kernels: none -> 68.3 us  [body(): pl.pallas_call(kernel, out_shape=(shape, shape), in_specs=[vmem] * 4 + [s...]
    all_to_all x10 -> x0, starting transfers between devices: 58.6 us -> none  [the longest x6 32 us: from_everyone(): lax.all_to_all(jnp.broadcast_to(shard[None], (peers, *shard.shape)), axis...]
    all_to_all x10 -> x0, waiting for transfers between devices: 47.4 us -> none  [the longest x6 32.2 us: from_everyone(): lax.all_to_all(jnp.broadcast_to(shard[None], (peers, *shard.shape)), axis...]
    gather x9 -> x0, local copies, waits for them, and re-layouts: 5.31 us -> none  [the longest x8 4.68 us: per_peer(): sources = parts[rows_one]]
    dynamic_update_slice x16 -> x0, local copies, waits for them, and re-layouts: 5.26 us -> none  [the longest x8 5.14 us: remote_terms(): return lax.map(per_peer, (tpos, tcore, None, rows), batch_size=4)]
    broadcast_in_dim x7 -> x0, local copies, waits for them, and re-layouts: 4.16 us -> none  [the longest x6 4.07 us: from_everyone(): jnp.broadcast_to(shard[None], (peers, *shard.shape))]
    unnamed x17 -> x13, local copies, waits for them, and re-layouts: 0.7 us -> 4.74 us
  transfers between devices with their start and end apart: 10 -> 0, of which waited for: 8 -> 0; matrix products, arithmetic and copies ran while one was open for 31% -> 0% of each run, Pallas kernels for 0% -> 0%
where the time goes in v1:
time: 74 us; the launch traced here: 73.7 us
  Pallas kernels  68.3 us (92%)
  local copies, waits for them, and re-layouts  4.74 us (6%)
    pallas_call x1, Pallas kernels, body(): pl.pallas_call(kernel, out_shape=(shape, shape), in_specs=[vmem] * 4 + [s...  68.3 us
    unnamed x13, local copies, waits for them, and re-layouts  4.74 us

profile of v1, /device:TPU:1, one launch (start us, length us, event | category | flops | bytes accessed | tf_op | source)
XLA Modules:
  0.0 73.7 jit_solution(7977259724011440115)
XLA Ops:
  0.6 0.0 copy-start.2
  0.6 0.0 copy-start.1
  0.6 0.7 copy-done.2
  1.3 0.7 copy.10.cen
  2.0 0.0 copy-done.1
  2.0 0.0 copy-start.3
  2.0 0.7 copy.11.sb
  2.7 0.0 copy-done.3
  2.7 0.7 copy.12.pr
  3.4 68.3 %vortex.1 = (f32[3,2048]{1,0:T(4,128)}, f32[3,2048]{1,0:T(4,128)}) custom-call(f32[3,2048]{1,0:T(4,128)} %pos.1, f32[3,2048]{1,0:T(4,128)} %strg.1, f32[16,128]{1,0:T(8,128)} %bitcast.2, s32[16,128]{1,0:T(8,128)} %bitcast.3, f32[3,2]{1,0:T(4,128)} %copy.10.cen, s32[16,4]{1,0:T(8,128)} %copy.11.sb, s32[64,2]{1,0:T(8,128)} %copy.12.pr, s32[16]{0:T(128)} %cnt.1), custom_call_target="tpu_custom_call" | custom-call | tf_op jit(solution)/shard_map/vortex/pallas_call | solution.py:483
  71.7 0.0 copy-start
  71.7 1.4 %copy.15 = f32[3,2048]{1,0:T(4,128)} copy(f32[3,2048]{1,0:T(4,128)} %get-tuple-element.4) | data formatting | bytes 49152
  73.0 0.0 copy-done
  73.0 0.6 copy.16
Async XLA Ops:
  0.6 0.7 copy-start.2
  0.6 1.4 %copy-start.1 = (s32[16,4]{0,1:T(4,128)S(1)}, s32[16,4]{0,1:T(4,128)}, u32[]{:S(2)}) copy-start(s32[16,4]{0,1:T(4,128)} %param.13) | copy-start | bytes 772
  2.0 0.7 copy-start.3
  71.7 1.4 %copy-start = (f32[3,2048]{1,0:T(4,128)S(1)}, f32[3,2048]{1,0:T(4,128)}, u32[]{:S(2)}) copy-start(f32[3,2048]{1,0:T(4,128)} %get-tuple-element.5) | copy-start | bytes 73732
